TPU v7x, 512 devices: a whole 4x4x16 slice. The times are simulated.
512 devices in a mesh: lon: 16 (over y, x_lo, core), lat: 32 (over x_hi, z).
Axes of the slice: x: 4 (x_hi: 2, x_lo: 2; x = x_hi * 2 + x_lo), y: 4, z: 16, core: 2. Of those that a mesh axis runs over, the one named last changes fastest.
Arguments:
- tokens: bfloat16 [256, 256, 768], P('lat', 'lon'), may hold values from -6 to 6
- patch_valid: int32 [256, 256], P('lat', 'lon'), may hold values 0 or 1
- block_mask: int32 [32, 16, 16], P('lat', 'lon'), may hold values from 0 to 1, as said below
- gain_attn: float32 [768], replicated, may hold values from 0.1 to 1.9
- gain_mlp: float32 [768], replicated, may hold values from 0.1 to 1.9
- w_qkv: bfloat16 [768, 2304], P('lat'), may hold values from -1.5 to 1.5
- w_out: bfloat16 [768, 768], P('lat'), may hold values from -0.21875 to 0.21875
- w_up: bfloat16 [768, 1536], P('lat'), may hold values from -0.21875 to 0.21875
- w_down: bfloat16 [1536, 768], P('lat'), may hold values from -0.15625 to 0.15625
Outputs:
- mixed: bfloat16 [256, 256, 768], P('lat', 'lon')
Inputs may be any that keep to these rules, and one draw needn't show every extreme that they name: block_mask[s, b, b] is 1 for every strip s and band b.
All inputs are finite; a program needn't handle non-finite values. No bound on the sum of `patch_valid` on one device may be relied on, other than what follows from the above.
Results may differ from a plain program's by a relative error of at most 0.013.
Values may be sent and summed in bfloat16 or wider, within the bound.
No kernel may reach another device: no remote copies, remote signals or barrier semaphores. Data moves between devices by JAX's collectives and lax.ppermute only.
A program may use at most 64 MiB of HBM per device.

v0:
```python
import jax
import jax.numpy as jnp
from jax import lax
from jax.sharding import PartitionSpec as P

D = 768
HEADS = 12
HEAD = 64
HALO = 2
MASKED = -1e30


def with_halo(block, sides, width):
    for axis, dim in sides:
        count = lax.axis_size(axis)
        forward = [(i, i + 1) for i in range(count - 1)]
        backward = [(target, source) for source, target in forward]
        low = lax.ppermute(
            lax.slice_in_dim(block, block.shape[dim] - width, None, axis=dim), axis, forward
        )
        high = lax.ppermute(lax.slice_in_dim(block, 0, width, axis=dim), axis, backward)
        block = jnp.concatenate([low, block, high], axis=dim)
    return block


def layer_norm(inputs, gain_vec):
    centre = jnp.mean(inputs, axis=-1, keepdims=True)
    spread = jnp.mean((inputs - centre) ** 2, axis=-1, keepdims=True)
    return (inputs - centre) * lax.rsqrt(spread + 1e-05) * gain_vec


def attend(running, queries, key_values, allowed):
    maxima, totals, weighted = running
    count_keys = key_values.shape[0]
    key_part = key_values[:, :D].reshape(count_keys, HEADS, HEAD)
    value_part = key_values[:, D:].reshape(count_keys, HEADS, HEAD)
    scores = jnp.einsum("qhd,khd->hqk", queries, key_part, preferred_element_type=jnp.float32)
    scores = jnp.where(allowed[None, None, :], scores, MASKED)
    new_max = jnp.maximum(maxima, jnp.max(scores, axis=-1))
    factor = jnp.exp(maxima - new_max)
    probs = jnp.where(allowed[None, None, :], jnp.exp(scores - new_max[..., None]), 0.0)
    totals = totals * factor + jnp.sum(probs, axis=-1)
    weighted = weighted * factor[..., None] + jnp.einsum(
        "hqk,khd->hqd", probs.astype(jnp.bfloat16), value_part, preferred_element_type=jnp.float32
    )
    return (new_max, totals, weighted)


def body(tokens, patch_valid, block_mask, gain_attn, gain_mlp, w_qkv, w_out, w_up, w_down):
    lat_rows, lon_cols = (tokens.shape[0], tokens.shape[1])
    tile_count = lat_rows * lon_cols
    full_qkv, full_out, full_up, full_down = (
        lax.all_gather(w_qkv, "lat", axis=0, tiled=True),
        lax.all_gather(w_out, "lat", axis=0, tiled=True),
        lax.all_gather(w_up, "lat", axis=0, tiled=True),
        lax.all_gather(w_down, "lat", axis=0, tiled=True),
    )
    residual_in = tokens.reshape(tile_count, D).astype(jnp.float32)
    normed = layer_norm(residual_in, gain_attn).astype(jnp.bfloat16)
    projected = jnp.dot(normed, full_qkv, preferred_element_type=jnp.float32)
    queries = (
        (projected[:, :D] * HEAD ** (-0.5)).astype(jnp.bfloat16).reshape(tile_count, HEADS, HEAD)
    )
    key_values = projected[:, D:].astype(jnp.bfloat16)
    kv_grid = key_values.reshape(lat_rows, lon_cols, 2 * D)
    padded = with_halo(kv_grid, (("lat", 0),), HALO)
    lat_place = lax.axis_index("lat")
    lat_count = lax.axis_size("lat")
    beside = jnp.concatenate([padded[:HALO], padded[lat_rows + HALO :]], axis=0).reshape(
        2 * HALO * lon_cols, 2 * D
    )
    beside_allowed = jnp.concatenate(
        [
            jnp.broadcast_to(lat_place > 0, (HALO * lon_cols,)),
            jnp.broadcast_to(lat_place < lat_count - 1, (HALO * lon_cols,)),
        ],
        axis=0,
    )
    running = (
        jnp.full((HEADS, tile_count), MASKED, jnp.float32),
        jnp.zeros((HEADS, tile_count), jnp.float32),
        jnp.zeros((HEADS, tile_count, HEAD), jnp.float32),
    )
    running = attend(running, queries, beside, beside_allowed)
    mask_row = block_mask.reshape(-1)
    band_total = mask_row.shape[0]
    portion = jax.tree.map(lambda a: lax.all_gather(a, "lon", axis=1, tiled=True), kv_grid)
    count_cols = portion.shape[1]
    channels = portion.shape[2]
    divisor = 1
    for candidate in range(min(count_cols, max(1, 1024 // lat_rows)), 0, -1):
        if count_cols % candidate == 0:
            divisor = candidate
            break
    groups = count_cols // divisor
    bands = (jnp.int32(0) + lax.iota(jnp.int32, count_cols)) // lon_cols
    hits = bands[:, None] == lax.iota(jnp.int32, band_total)[None, :]
    col_ok = (jnp.sum(jnp.where(hits, mask_row[None, :], 0), axis=1) > 0).reshape(groups, divisor)
    blocks = jnp.moveaxis(portion.reshape(lat_rows, groups, divisor, channels), 1, 0)

    def advance(state_now, item):
        block, block_ok = item
        flattened = block.reshape(lat_rows * divisor, channels)
        key_ok = jnp.broadcast_to(block_ok[None, :], (lat_rows, divisor)).reshape(-1)
        return (attend(state_now, queries, flattened, key_ok), None)

    state_out, unused = lax.scan(advance, running, (blocks, col_ok))
    running = state_out
    maxima, totals, weighted = running
    context = weighted / totals[..., None]
    context = jnp.transpose(context, (1, 0, 2)).reshape(tile_count, D).astype(jnp.bfloat16)
    validity = patch_valid.reshape(tile_count, 1).astype(jnp.float32)
    attended = jnp.dot(context, full_out, preferred_element_type=jnp.float32)
    hidden_state = (residual_in + validity * attended).astype(jnp.bfloat16)
    residual = hidden_state.astype(jnp.float32)
    normed_two = layer_norm(residual, gain_mlp).astype(jnp.bfloat16)
    inner = jax.nn.gelu(jnp.dot(normed_two, full_up, preferred_element_type=jnp.float32)).astype(
        jnp.bfloat16
    )
    mixed = residual + validity * jnp.dot(inner, full_down, preferred_element_type=jnp.float32)
    return mixed.astype(jnp.bfloat16).reshape(lat_rows, lon_cols, D)


def solution(mesh):
    in_specs = (
        P("lat", "lon", None),
        P("lat", "lon"),
        P("lat", "lon", None),
        P(),
        P(),
        P("lat", None),
        P("lat", None),
        P("lat", None),
        P("lat", None),
    )
    out_specs = P("lat", "lon", None)
    return jax.shard_map(body, mesh=mesh, in_specs=in_specs, out_specs=out_specs, check_vma=False)
```

profile of v0, /device:TPU:8, one launch (start us, length us, event | category | flops | bytes accessed | tf_op | source)
XLA Modules:
  0.0 680.6 jit_solution(9554029814059372410)
XLA Ops:
  10.8 164.0 %all-gather.6.cloned.1.call-done = bf16[768,2304]{1,0:T(8,128)(2,1)} async-done(((bf16[24,2304]{1,0:T(8,128)(2,1)}), bf16[768,2304]{1,0:T(8,128)(2,1)}) %all-gather.6.cloned.1.call-update) | async-done | bytes 3538960 | tf_op jit(solution)/shard_map/all_gather | solution.py:53
  174.7 2.6 fusion.58
  181.5 3.7 collective-permute-start
  185.2 1.3 collective-permute-start.1
  187.4 4.3 collective-permute-done.1
  194.0 29.0 %all-gather.8.cloned.1.call-done = bf16[8,256,1536]{2,1,0:T(8,128)(2,1)} async-done(((bf16[8,16,1536]{2,1,0:T(8,128)(2,1)}), bf16[8,256,1536]{2,1,0:T(8,128)(2,1)}) %all-gather.8.cloned.1.call-update) | async-done | bytes 6291472 | tf_op jit(solution)/shard_map/all_gather | solution.py:87
  223.0 35.1 %while.14 = (s32[]{:T(128)}, f32[12,128]{1,0:T(8,128)S(1)}, f32[12,128]{1,0:T(8,128)}, f32[12,128,64]{1,2,0:T(8,128)}, pred[2,128]{1,0:T(4,128)(4,1)}, /*index=5...) while((s32[]{:T(128)}, f32[12,128]{1,0:T(8,128)S(1)}, f32[12,128]{1,0:T(8,128)}, ...), condition=%wide.region_8.9_spmd, body=%wide.region_5.8_spmd.sunk | while | flops 418581504 | bytes 67224168 | solution.py:107
  223.7 2.1 constant_dynamic-slice_fusion.2
  225.9 1.4 fusion.83
  227.2 1.7 copy.35
  228.9 1.4 bitcast_reduce_fusion.2
  230.4 2.5 fusion.84
  235.0 5.6 fusion.85
  241.3 2.1 constant_dynamic-slice_fusion.2
  243.4 1.4 fusion.83
  244.8 1.7 copy.35
  246.5 1.4 bitcast_reduce_fusion.2
  248.0 2.5 fusion.84
  252.6 5.6 fusion.85
  259.2 112.0 %all-gather.10.cloned.1.call-done = bf16[768,768]{1,0:T(8,128)(2,1)} async-done(((bf16[24,768]{1,0:T(8,128)(2,1)}), bf16[768,768]{1,0:T(8,128)(2,1)}) %all-gather.10.cloned.1.call-update) | async-done | bytes 1179664 | tf_op jit(solution)/shard_map/all_gather | solution.py:54
  371.2 1.7 fusion.60
  373.2 147.3 %all-gather.12.cloned.1.call-done = bf16[768,1536]{1,0:T(8,128)(2,1)} async-done(((bf16[24,1536]{1,0:T(8,128)(2,1)}), bf16[768,1536]{1,0:T(8,128)(2,1)}) %all-gather.12.cloned.1.call-update) | async-done | bytes 2359312 | tf_op jit(solution)/shard_map/all_gather | solution.py:55
  520.4 149.6 %all-gather.14.cloned.1.call-done = bf16[1536,768]{1,0:T(8,128)(2,1)} async-done(((bf16[48,768]{1,0:T(8,128)(2,1)}), bf16[1536,768]{1,0:T(8,128)(2,1)}) %all-gather.14.cloned.1.call-update) | async-done | bytes 2359312 | tf_op jit(solution)/shard_map/all_gather | solution.py:56
  670.0 4.1 fusion.17
  (84 shorter events, 18.1 us)
Async XLA Ops:
  6.5 168.2 %all-gather.6.cloned.1.call-start = ((), (), s32[]{:S(2)}) async-start(), calls=%async_computation | async-start | bytes 3649536 | tf_op jit(solution)/shard_map/all_gather | solution.py:53
  7.3 215.8 %all-gather.8.cloned.1.call-start = ((), (), s32[]{:S(2)}) async-start(), calls=%async_computation.1 | async-start | bytes 6684672 | tf_op jit(solution)/shard_map/all_gather | solution.py:87
  10.7 169.4 %copy-start.8 = (s32[1,1,16]{2,1,0:T(1,128)S(1)}, s32[1,1,16]{2,1,0:T(1,128)}, u32[]{:S(2)}) copy-start(s32[1,1,16]{2,1,0:T(1,128)} %param.13) | copy-start | bytes 196
  10.8 170.0 %copy-start.6 = (s32[8,16]{1,0:T(8,128)S(1)}, s32[8,16]{1,0:T(8,128)}, u32[]{:S(2)}) copy-start(s32[8,16]{1,0:T(8,128)} %param.12) | copy-start | bytes 1540
  178.2 193.0 %all-gather.10.cloned.1.call-start = ((), (), s32[]{:S(2)}) async-start(), calls=%async_computation.2 | async-start | bytes 1216512 | tf_op jit(solution)/shard_map/all_gather | solution.py:54
  178.9 341.5 %all-gather.12.cloned.1.call-start = ((), (), s32[]{:S(2)}) async-start(), calls=%async_computation.3 | async-start | bytes 2433024 | tf_op jit(solution)/shard_map/all_gather | solution.py:55
  179.5 490.5 %all-gather.14.cloned.1.call-start = ((), (), s32[]{:S(2)}) async-start(), calls=%async_computation.4 | async-start | bytes 2433024 | tf_op jit(solution)/shard_map/all_gather | solution.py:56
  181.5 5.9 collective-permute-start
  185.2 6.5 collective-permute-start.1
  223.0 148.2 %copy-start.1 = (bf16[8,16,768]{2,1,0:T(8,128)(2,1)S(1)}, bf16[8,16,768]{2,1,0:T(8,128)(2,1)}, u32[]{:S(2)}) copy-start(bf16[8,16,768]{2,1,0:T(8,128)(2,1)} %param.11) | copy-start | bytes 589828
  223.7 5.2 copy-start.4
  230.4 2.7 copy-start
  230.4 2.6 copy-start.2
  233.7 0.6 copy-start.3
  233.7 1.4 copy-start.5
  241.3 5.2 copy-start.4
  247.9 2.7 copy-start
  247.9 2.6 copy-start.2
  251.2 0.6 copy-start.3
  251.2 1.4 copy-start.5
  258.1 411.9 %copy-start.7 = (f32[128]{0:T(128)S(1)}, f32[128]{0:T(128)}, u32[]{:S(2)}) copy-start(f32[128]{0:T(128)} %convert_element_type.61) | copy-start | bytes 1540
  258.1 411.9 %copy-start.9 = (f32[768]{0:T(1024)S(1)}, f32[768]{0:T(1024)}, u32[]{:S(2)}) copy-start(f32[768]{0:T(1024)} %param.15) | copy-start | bytes 9220
Sparse Core Ops, SparseCore 0:
  10.5 164.2 all-gather.5
  178.3 44.6 all-gather.7
  226.1 145.0 all-gather.9
  374.2 146.2 all-gather.11
  523.4 146.6 all-gather.13
where the time goes:
time: 681 us
  waiting for transfers between devices  609 us (89%)
  matrix products  23.7 us (3%)
  local copies, waits for them, and re-layouts  16.8 us (2%)
  between operations  13.3 us (2%)
  other arithmetic  12.3 us (2%)
    all_gather x1, waiting for transfers between devices, body(): lax.all_gather(w_qkv, 'lat', axis=0, tiled=True)  164 us
    all_gather x1, waiting for transfers between devices, body(): lax.all_gather(w_down, 'lat', axis=0, tiled=True)  150 us
    all_gather x1, waiting for transfers between devices, body(): lax.all_gather(w_up, 'lat', axis=0, tiled=True)  147 us
    all_gather x1, waiting for transfers between devices, body(): lax.all_gather(w_out, 'lat', axis=0, tiled=True)  112 us
    all_gather x1, waiting for transfers between devices, body(): lax.all_gather(a, 'lon', axis=1, tiled=True)  29 us
  transfers between devices with their start and end apart: 7, of which 7 were waited for; matrix products, arithmetic and copies ran while one was open for 6% of the time, Pallas kernels for 0%

commit v1 on v0

--- a/solution.py
+++ b/solution.py
@@ -8,6 +8,13 @@
 HEAD = 64
 HALO = 2
 MASKED = -1e30
+
+
+def all_by_exchange(x, axis, along):
+    devices = lax.axis_size(axis)
+    pieces = jnp.stack([x for _ in range(devices)])
+    pieces = lax.all_to_all(pieces, axis, split_axis=0, concat_axis=0)
+    return jnp.concatenate(pieces, axis=along)
 
 
 def with_halo(block, sides, width):
@@ -52,7 +59,7 @@
     full_qkv, full_out, full_up, full_down = (
         lax.all_gather(w_qkv, "lat", axis=0, tiled=True),
         lax.all_gather(w_out, "lat", axis=0, tiled=True),
-        lax.all_gather(w_up, "lat", axis=0, tiled=True),
+        all_by_exchange(w_up, "lat", 0),
         lax.all_gather(w_down, "lat", axis=0, tiled=True),
     )
     residual_in = tokens.reshape(tile_count, D).astype(jnp.float32)

time: 681 us -> 549 us (0.81)
  waiting for transfers between devices: 609 us -> 469 us
  starting transfers between devices: 5.11 us -> 13.1 us
    all_gather x1 -> x0, waiting for transfers between devices: 147 us -> none  [body(): lax.all_gather(w_up, 'lat', axis=0, tiled=True)]
    ppermute x1, waiting for transfers between devices: 0.69 us -> 85.9 us  [with_halo(): lax.ppermute(lax.slice_in_dim(block, block.shape[dim] - width, None, axis...]
    all_gather x1, waiting for transfers between devices: 112 us -> 66.9 us  [body(): lax.all_gather(w_out, 'lat', axis=0, tiled=True)]
    all_gather x1, waiting for transfers between devices: 29 us -> 0.01 us  [body(): lax.all_gather(a, 'lon', axis=1, tiled=True)]
    all_to_all x0 -> x1, starting transfers between devices: none -> 8.05 us  [all_by_exchange(): pieces = lax.all_to_all(pieces, axis, split_axis=0, concat_axis=0)]
  transfers between devices with their start and end apart: 7 -> 7, of which waited for: 7 -> 5; matrix products, arithmetic and copies ran while one was open for 6% -> 8% of each run, Pallas kernels for 0% -> 0%
where the time goes in v1:
time: 549 us
  waiting for transfers between devices  469 us (85%)
  matrix products  23.1 us (4%)
  local copies, waits for them, and re-layouts  18.4 us (3%)
  between operations  13.3 us (2%)
  starting transfers between devices  13.1 us (2%)
  other arithmetic  12 us (2%)
    all_gather x1, waiting for transfers between devices, body(): lax.all_gather(w_qkv, 'lat', axis=0, tiled=True)  164 us
    all_gather x1, waiting for transfers between devices, body(): lax.all_gather(w_down, 'lat', axis=0, tiled=True)  147 us
    ppermute x1, waiting for transfers between devices, with_halo(): lax.ppermute(lax.slice_in_dim(block, block.shape[dim] - width, None, axis...  85.9 us
    all_gather x1, waiting for transfers between devices, body(): lax.all_gather(w_out, 'lat', axis=0, tiled=True)  66.9 us
    dot_general x3, matrix products, attend(): jnp.einsum('hqk,khd->hqd', probs.astype(jnp.bfloat16), value_part, prefer...  11.6 us
  transfers between devices with their start and end apart: 7, of which 5 were waited for; matrix products, arithmetic and copies ran while one was open for 8% of the time, Pallas kernels for 0%

profile of v1, /device:TPU:8, one launch (start us, length us, event | category | flops | bytes accessed | tf_op | source)
XLA Modules:
  0.0 548.8 jit_solution(6821103623028189184)
XLA Ops:
  10.8 164.0 %all-gather.5.cloned.1.call-done = bf16[768,2304]{1,0:T(8,128)(2,1)} async-done(((bf16[24,2304]{1,0:T(8,128)(2,1)}), bf16[768,2304]{1,0:T(8,128)(2,1)}) %all-gather.5.cloned.1.call-update) | async-done | bytes 3538960 | tf_op jit(solution)/shard_map/all_gather | solution.py:60
  174.7 2.6 fusion.58
  179.0 1.6 stack.2
  180.5 8.0 %all-to-all-start = ((bf16[32,24,1536]{2,1,0:T(8,128)(2,1)}), bf16[32,24,1536]{2,1,0:T(8,128)(2,1)}, u32[]{:S(2)}, u32[]{:S(2)}) async-start(bf16[32,24,1536]{2,1,0:T(8,128)(2,1)} %stack.2), calls=%async_computation | async-start | bytes 4718592 | tf_op jit(solution)/shard_map/all_to_all | solution.py:16
  190.5 3.6 collective-permute-start
  195.6 85.9 %collective-permute-done = bf16[2,16,1536]{2,1,0:T(8,128)(2,1)S(1)} collective-permute-done((bf16[2,16,1536]{2,1,0:T(8,128)(2,1)S(1)}, bf16[2,16,1536]{2,1,0:T(8,128)(2,1)S(1)}, u32[]{:S(2)}, u32[]{:S(2)}) %collective-permute-start) | collective-permute-done | bytes 98336 | tf_op jit(solution)/shard_map/ppermute | solution.py:25
  281.5 2.7 collective-permute-done.1
  286.6 34.4 %while.14 = (s32[]{:T(128)}, f32[12,128]{1,0:T(8,128)S(1)}, f32[12,128]{1,0:T(8,128)}, f32[12,128,64]{1,2,0:T(8,128)}, pred[2,128]{1,0:T(4,128)(4,1)}, /*index=5...) while((s32[]{:T(128)}, f32[12,128]{1,0:T(8,128)S(1)}, f32[12,128]{1,0:T(8,128)}, ...), condition=%wide.region_8.9_spmd, body=%wide.region_5.8_spmd.sunk | while | flops 418581504 | bytes 67224168 | solution.py:114
  287.3 2.1 constant_dynamic-slice_fusion.2
  289.4 1.4 fusion.83
  290.7 1.7 copy.35
  292.5 1.4 bitcast_reduce_fusion.2
  294.0 2.5 fusion.84
  298.5 5.3 fusion.85
  304.5 2.1 constant_dynamic-slice_fusion.2
  306.6 1.4 fusion.83
  307.9 1.7 copy.35
  309.7 1.4 bitcast_reduce_fusion.2
  311.1 2.5 fusion.84
  315.7 5.3 fusion.85
  322.1 66.9 %all-gather.9.cloned.1.call-done = bf16[768,768]{1,0:T(8,128)(2,1)} async-done(((bf16[24,768]{1,0:T(8,128)(2,1)}), bf16[768,768]{1,0:T(8,128)(2,1)}) %all-gather.9.cloned.1.call-update) | async-done | bytes 1179664 | tf_op jit(solution)/shard_map/all_gather | solution.py:61
  389.0 1.7 fusion.60
  390.9 147.3 %all-gather.11.cloned.1.call-done = bf16[1536,768]{1,0:T(8,128)(2,1)} async-done(((bf16[48,768]{1,0:T(8,128)(2,1)}), bf16[1536,768]{1,0:T(8,128)(2,1)}) %all-gather.11.cloned.1.call-update) | async-done | bytes 2359312 | tf_op jit(solution)/shard_map/all_gather | solution.py:63
  538.2 4.1 fusion.17
  (86 shorter events, 18.1 us)
Async XLA Ops:
  6.5 168.2 %all-gather.5.cloned.1.call-start = ((), (), s32[]{:S(2)}) async-start(), calls=%async_computation.1 | async-start | bytes 3649536 | tf_op jit(solution)/shard_map/all_gather | solution.py:60
  7.3 279.4 %all-gather.7.cloned.1.call-start = ((), (), s32[]{:S(2)}) async-start(), calls=%async_computation.2 | async-start | bytes 6684672 | tf_op jit(solution)/shard_map/all_gather | solution.py:94
  10.7 168.2 %copy-start.6 = (bf16[24,1536]{1,0:T(8,128)(2,1)S(1)}, bf16[24,1536]{1,0:T(8,128)(2,1)}, u32[]{:S(2)}) copy-start(bf16[24,1536]{1,0:T(8,128)(2,1)} %param.18) | copy-start | bytes 221188
  178.2 210.8 %all-gather.9.cloned.1.call-start = ((), (), s32[]{:S(2)}) async-start(), calls=%async_computation.3 | async-start | bytes 1216512 | tf_op jit(solution)/shard_map/all_gather | solution.py:61
  180.5 8.7 %copy-start.7 = (s32[8,16]{1,0:T(8,128)S(1)}, s32[8,16]{1,0:T(8,128)}, u32[]{:S(2)}) copy-start(s32[8,16]{1,0:T(8,128)} %param.12) | copy-start | bytes 1540
  180.5 9.3 %copy-start.9 = (s32[1,1,16]{2,1,0:T(1,128)S(1)}, s32[1,1,16]{2,1,0:T(1,128)}, u32[]{:S(2)}) copy-start(s32[1,1,16]{2,1,0:T(1,128)} %param.13) | copy-start | bytes 196
  180.5 357.7 %all-to-all-start = ((bf16[32,24,1536]{2,1,0:T(8,128)(2,1)}), bf16[32,24,1536]{2,1,0:T(8,128)(2,1)}, u32[]{:S(2)}, u32[]{:S(2)}) async-start(bf16[32,24,1536]{2,1,0:T(8,128)(2,1)} %stack.2), calls=%async_computation | async-start | bytes 4718592 | tf_op jit(solution)/shard_map/all_to_all | solution.py:16
  188.6 349.6 %all-gather.11.cloned.1.call-start = ((), (), s32[]{:S(2)}) async-start(), calls=%async_computation.4 | async-start | bytes 2433024 | tf_op jit(solution)/shard_map/all_gather | solution.py:63
  190.5 91.1 %collective-permute-start = (bf16[2,16,1536]{2,1,0:T(8,128)(2,1)S(1)}, bf16[2,16,1536]{2,1,0:T(8,128)(2,1)S(1)}, u32[]{:S(2)}, u32[]{:S(2)}) collective-permute-start(bf16[2,16,1536]{2,1,0:T(8,128)(2,1)S(1)} %bitcast.92), channel_id=1, source_target_pairs={{0,1},{1,2},{2,3},{3,4},{4,5},{5,6},{6,7},{7,8},{8,9},{9,10},{10,1... | collective-permute-start | bytes 294920 | tf_op jit(solution)/shard_map/ppermute | solution.py:25
  194.1 90.1 %collective-permute-start.1 = (bf16[2,16,1536]{2,1,0:T(8,128)(2,1)S(1)}, bf16[2,16,1536]{2,1,0:T(8,128)(2,1)S(1)}, u32[]{:S(2)}, u32[]{:S(2)}) collective-permute-start(bf16[2,16,1536]{2,1,0:T(8,128)(2,1)S(1)} %bitcast.91), channel_id=1, source_target_pairs={{1,0},{2,1},{3,2},{4,3},{5,4},{6,5},{7,6},{8,7},{9,8},{10,9},{11,1... | collective-permute-start | bytes 294920 | tf_op jit(solution)/shard_map/ppermute | solution.py:28
  286.6 102.4 %copy-start.1 = (bf16[8,16,768]{2,1,0:T(8,128)(2,1)S(1)}, bf16[8,16,768]{2,1,0:T(8,128)(2,1)}, u32[]{:S(2)}) copy-start(bf16[8,16,768]{2,1,0:T(8,128)(2,1)} %param.11) | copy-start | bytes 589828
  287.3 5.2 copy-start.4
  293.9 2.7 copy-start
  293.9 2.6 copy-start.2
  297.2 0.6 copy-start.3
  297.2 1.4 copy-start.5
  304.4 5.2 copy-start.4
  311.1 2.7 copy-start
  311.1 2.6 copy-start.2
  314.4 0.6 copy-start.3
  314.4 1.4 copy-start.5
  321.0 217.2 %copy-start.8 = (f32[128]{0:T(128)S(1)}, f32[128]{0:T(128)}, u32[]{:S(2)}) copy-start(f32[128]{0:T(128)} %convert_element_type.61) | copy-start | bytes 1540
  321.0 217.2 %copy-start.10 = (f32[768]{0:T(1024)S(1)}, f32[768]{0:T(1024)}, u32[]{:S(2)}) copy-start(f32[768]{0:T(1024)} %param.15) | copy-start | bytes 9220
Sparse Core Ops, SparseCore 0:
  10.5 164.2 all-gather.4
  178.3 51.2 all-gather.6
  232.8 156.1 all-gather.8
  391.9 146.2 all-gather.10
